TPU v7x, 32 devices: a whole 2x2x4 slice. The times are simulated.
32 devices in a mesh: qa: 4 (over y, x), qb: 8 (over z, core).
Axes of the slice: x: 2, y: 2, z: 4, core: 2. Of those that a mesh axis runs over, the one named last changes fastest.
Arguments:
- amplitudes: float32 [2, 2097152], P(None, ('qa', 'qb')), may hold values from -6 to 6
- gate_blocks: float32 [4, 6, 2, 128, 128], replicated, may hold values from -0.375 to 0.375
- phase_low: float32 [4, 256], replicated, may hold values from -3.140625 to 3.140625
- phase_high: float32 [4, 256], replicated, may hold values from -3.140625 to 3.140625
- phase_global: float32 [4, 4, 8], P(None, 'qa', 'qb'), may hold values from -3.140625 to 3.140625
Outputs:
- final_state: float32 [2, 2097152], P(None, ('qa', 'qb'))
All inputs are finite; a program needn't handle non-finite values.
Results may differ from a plain program's by a relative error of at most 0.00011.
Values sent between devices are 32-bit elements; how exact they have to be, the bound alone decides.
No kernel may reach another device: no remote copies, remote signals or barrier semaphores. Data moves between devices by JAX's collectives and lax.ppermute only.
A program may use at most 64 MiB of HBM per device.

v0:
```python
import jax
import jax.numpy as jnp
from jax import lax
from jax.sharding import PartitionSpec as P


def apply_gate(state, matrix, where):
    width = matrix.shape[-1]
    cells = state.shape[2]
    stacked = jnp.concatenate([matrix[0], matrix[1]], axis=0)
    if where == 0:
        values = state.reshape(2 * (cells // width), width)
        product = lax.dot_general(
            values, stacked, (((1,), (1,)), ((), ())), precision=lax.Precision.HIGHEST
        )
        product = product.reshape(2, cells // width, 2, width)
        out_real = product[0, :, 0] - product[1, :, 1]
        out_imag = product[0, :, 1] + product[1, :, 0]
    elif where == 1:
        upper = cells // (width * width)
        values = state.reshape(2, upper, width, width)
        product = lax.dot_general(
            stacked, values, (((1,), (2,)), ((), ())), precision=lax.Precision.HIGHEST
        )
        product = product.reshape(2, width, 2, upper, width)
        out_real = jnp.transpose(product[0, :, 0] - product[1, :, 1], (1, 0, 2))
        out_imag = jnp.transpose(product[1, :, 0] + product[0, :, 1], (1, 0, 2))
    else:
        values = state.reshape(2, width, cells // width)
        product = lax.dot_general(
            stacked, values, (((1,), (1,)), ((), ())), precision=lax.Precision.HIGHEST
        )
        product = product.reshape(2, width, 2, cells // width)
        out_real = product[0, :, 0] - product[1, :, 1]
        out_imag = product[1, :, 0] + product[0, :, 1]
    return jnp.stack([out_real.reshape(cells), out_imag.reshape(cells)]).reshape(2, 1, cells)


def apply_phase(state, low_angles, high_angles, global_angles):
    local = (high_angles[:, None] + low_angles[None, :]).reshape(-1)
    theta = global_angles.reshape(-1, 1) + local[None, :]
    cosine = jnp.cos(theta)
    sine = jnp.sin(theta)
    return jnp.stack([state[0] * cosine - state[1] * sine, state[0] * sine + state[1] * cosine])


def regroup_with_gate(state, which, matrix):
    cells = state.shape[2]
    width = matrix.shape[-1]

    def lowest_gate(pieces):
        shape = pieces.shape
        flat = pieces.reshape(2, 1, shape[1] * shape[2] * shape[3])
        return apply_gate(flat, matrix, 0).reshape(shape)

    if which == 0:
        count = lax.axis_size("qa")
        blocks = state.reshape(2, count, cells // (count * width), width)
        moved = lowest_gate(lax.all_to_all(blocks, "qa", split_axis=1, concat_axis=1, tiled=True))
    else:
        count = lax.axis_size("qb")
        blocks = state.reshape(2, count, cells // (count * width), width)
        moved = lowest_gate(lax.all_to_all(blocks, "qb", split_axis=1, concat_axis=1, tiled=True))
    return moved.reshape(2, 1, cells)


def body(amplitudes, gate_blocks, phase_low, phase_high, phase_global):
    cells = amplitudes.shape[1]
    state = amplitudes.reshape(2, 1, cells)
    segments = gate_blocks.shape[0]
    per_segment = gate_blocks.shape[1]
    done_lowest = False
    for segment in range(segments):
        for gate in range(per_segment):
            if gate == 0 and done_lowest:
                continue
            state = apply_gate(state, gate_blocks[segment, gate], gate % 3)
        done_lowest = False
        state = apply_phase(
            state, phase_low[segment], phase_high[segment], phase_global[segment].reshape(1)
        )
        if segment < 3:
            which = 1 if segment == 1 else 0
            state = regroup_with_gate(state, which, gate_blocks[segment + 1, 0])
            done_lowest = True
    return state.reshape(2, cells)


def solution(mesh):
    return jax.shard_map(
        body,
        mesh=mesh,
        in_specs=(P(None, ("qa", "qb")), P(), P(), P(), P(None, "qa", "qb")),
        out_specs=P(None, ("qa", "qb")),
        check_vma=False,
    )
```

profile of v0, /device:TPU:0, one launch (start us, length us, event | category | flops | bytes accessed | tf_op | source)
XLA Modules:
  0.0 91.7 jit_solution(12786966690081837345)
XLA Ops:
  0.0 2.2 %slice_bitcast_fusion.3 = (f32[128,128]{1,0:T(8,128)S(1)}, f32[128,128]{1,0:T(8,128)S(1)}, f32[128,128]{1,0:T(8,128)S(1)}, f32[128,128]{1,0:T(8,128)S(1)}, f32[1...) fusion(f32[4,6,2,128,128]{4,3,2,1,0:T(8,128)} %param.6), kind=kLoop, calls=%fused_computation.214 | loop fusion | bytes 2490368 | tf_op jit(solution)/shard_map/squeeze | solution.py:10
  2.2 2.1 %slice_bitcast_fusion.21 = (f32[128,128]{1,0:T(8,128)}, f32[128,128]{1,0:T(8,128)}, f32[128,128]{1,0:T(8,128)}, f32[128,128]{1,0:T(8,128)S(1)}, f32[128,128]{1,0...) fusion(f32[4,6,2,128,128]{4,3,2,1,0:T(8,128)} %param.6), kind=kLoop, calls=%fused_computation.232 | loop fusion | bytes 2490368 | tf_op jit(solution)/shard_map/squeeze | solution.py:10
  4.8 1.9 %convolution_bitcast_fusion = f32[1024,256]{0,1:T(8,128)S(1)} fusion(f32[1024,128]{1,0:T(8,128)S(1)} %reshape_reshape.2, f32[128,128]{1,0:T(8,128)} %get-tuple-element.20, f32[128,128]{1,0:T(8,128)} %get-tuple-element.21), kind=kOutput, calls=%fused_computation | convolution fusion | flops 402685952 | bytes 1703936 | tf_op jit(solution)/shard_map/dot_general | solution.py:13
  11.8 1.0 %fusion.6 = f32[2,512,2,128]{3,1,2,0:T(8,128)S(1)} fusion(f32[2,128,128,1]{2,1,0,3:T(8,128)S(1)} %bitcast.577, f32[1,512,128]{2,1,0:T(8,128)S(1)} %add.620, f32[1,512,128]{2,1,0:T(8,128)S(1)} %sub.362), kind=kOutput, calls=%fused_computation.10 | convolution fusion | flops 402784256 | bytes 1703936 | tf_op jit(solution)/shard_map/dot_general | solution.py:13
  14.1 1.0 %fusion.12 = f32[2,128,2,512]{3,1,2,0:T(8,128)S(1)} fusion(f32[2,128,128,1]{2,1,3,0:T(8,128)S(1)} %bitcast.573, f32[1,128,512]{2,1,0:T(8,128)S(1)} %stack.123, f32[1,128,512]{2,1,0:T(8,128)S(1)} %stack.122), kind=kOutput, calls=%fused_computation.18 | convolution fusion | flops 402784256 | bytes 1703936 | tf_op jit(solution)/shard_map/dot_general | solution.py:30
  16.3 1.8 %fusion.82 = (f32[1,4,128,128]{3,2,0,1:T(8,128)S(1)}, f32[1,4,128,128]{3,2,0,1:T(8,128)S(1)}) fusion(f32[1,4,128,128]{3,2,1,0:T(8,128)S(1)} %add.638, f32[1,4,128,128]{3,2,1,0:T(8,128)S(1)} %sub.368, f32[128,128]{1,0:T(8,128)S(1)} %bitcast.579, f32[4,128]{1,0:T(4,128)S(1)} %copy.27, f32[]{:T(128)} %bitcast.106), kind=kLoop, calls=%fused_computation.169 | loop fusion | flops 524288 | bytes 1116164 | tf_op jit(solution)/shard_map/sub | solution.py:44
  18.9 5.2 %all-to-all-start = ((f32[2,4,128,128]{3,2,0,1:T(8,128)}), f32[2,4,128,128]{3,2,0,1:T(8,128)S(1)}, u32[]{:S(2)}, u32[]{:S(2)}) async-start(f32[2,4,128,128]{3,2,0,1:T(8,128)} %pad_maximum_fusion), calls=%async_computation | async-start | bytes 1048576 | tf_op jit(solution)/shard_map/all_to_all | solution.py:59
  24.7 7.4 %all-to-all-done = f32[2,4,128,128]{3,2,0,1:T(8,128)S(1)} async-done(((f32[2,4,128,128]{3,2,0,1:T(8,128)}), f32[2,4,128,128]{3,2,0,1:T(8,128)S(1)}, u32[]{:S(2)}, u32[]{:S(2)}) %all-to-all-start) | async-done | bytes 524320 | tf_op jit(solution)/shard_map/all_to_all | solution.py:59
  32.2 1.0 %fusion.118 = f32[2,512,2,128]{3,1,2,0:T(8,128)S(1)} fusion(f32[2,512,128,1]{2,1,3,0:T(8,128)S(1)} %bitcast.536, f32[2,128,128,1]{2,1,0,3:T(8,128)S(1)} %bitcast.559), kind=kOutput, calls=%fused_computation.285 | convolution fusion | flops 402653184 | bytes 1703936 | tf_op jit(solution)/shard_map/dot_general | solution.py:13
  35.5 1.0 %fusion.21 = f32[2,512,2,128]{3,1,2,0:T(8,128)S(1)} fusion(f32[2,128,128,1]{2,1,0,3:T(8,128)S(1)} %bitcast.560, f32[1,512,128]{2,1,0:T(8,128)S(1)} %add.645, f32[1,512,128]{2,1,0:T(8,128)S(1)} %sub.375), kind=kOutput, calls=%fused_computation.31 | convolution fusion | flops 402784256 | bytes 1703936 | tf_op jit(solution)/shard_map/dot_general | solution.py:13
  38.9 1.7 %fusion.80 = (f32[1,8,64,128]{3,2,0,1:T(8,128)S(1)}, f32[1,8,64,128]{3,2,0,1:T(8,128)S(1)}) fusion(f32[1,8,64,128]{3,2,1,0:T(8,128)S(1)} %add.663, f32[1,8,64,128]{3,2,1,0:T(8,128)S(1)} %sub.381, f32[64,128]{1,0:T(8,128)S(1)} %bitcast.582, f32[8,64]{1,0:T(8,128)S(1)} %copy.34, f32[]{:T(128)} %bitcast.143), kind=kLoop, calls=%fused_computation.163 | loop fusion | flops 524288 | bytes 1083396 | tf_op jit(solution)/shard_map/sub | solution.py:44
  41.5 4.9 %all-to-all-start.1 = ((f32[2,8,64,128]{3,2,0,1:T(8,128)}), f32[2,8,64,128]{3,2,0,1:T(8,128)S(1)}, u32[]{:S(2)}, u32[]{:S(2)}) async-start(f32[2,8,64,128]{3,2,0,1:T(8,128)} %pad_maximum_fusion.1), calls=%async_computation.1 | async-start | bytes 1048576 | tf_op jit(solution)/shard_map/all_to_all | solution.py:63
  46.4 1.6 %fusion.84 = (f32[256,256]{1,0:T(8,128)S(1)}, f32[256,256]{1,0:T(8,128)S(1)}) fusion(f32[256]{0:T(256)S(1)} %bitcast.586, f32[256]{0:T(256)S(1)} %bitcast.585, f32[]{:T(128)} %bitcast.217), kind=kLoop, calls=%fused_computation.174 | loop fusion | flops 131072 | bytes 526340 | tf_op jit(solution)/shard_map/sin | solution.py:43
  48.1 1.2 %slice_bitcast_fusion.41 = (f32[128,128]{1,0:T(8,128)S(1)}, f32[128,128]{1,0:T(8,128)S(1)}, f32[128,128]{1,0:T(8,128)S(1)}, f32[128,128]{1,0:T(8,128)S(1)}, f32[...) fusion(f32[4,6,2,128,128]{4,3,2,1,0:T(8,128)} %param.6), kind=kLoop, calls=%fused_computation.252 | loop fusion | bytes 1310720 | tf_op jit(solution)/shard_map/squeeze | solution.py:10
  49.2 12.4 %all-to-all-done.1 = f32[2,8,64,128]{3,2,0,1:T(8,128)S(1)} async-done(((f32[2,8,64,128]{3,2,0,1:T(8,128)}), f32[2,8,64,128]{3,2,0,1:T(8,128)S(1)}, u32[]{:S(2)}, u32[]{:S(2)}) %all-to-all-start.1) | async-done | bytes 524320 | tf_op jit(solution)/shard_map/all_to_all | solution.py:63
  61.7 1.0 %fusion.119 = f32[2,512,2,128]{3,1,2,0:T(8,128)S(1)} fusion(f32[2,512,128,1]{2,1,3,0:T(8,128)S(1)} %bitcast.537, f32[2,128,128,1]{2,1,0,3:T(8,128)S(1)} %bitcast.557), kind=kOutput, calls=%fused_computation.286 | convolution fusion | flops 402653184 | bytes 1703936 | tf_op jit(solution)/shard_map/dot_general | solution.py:13
  65.1 1.0 %fusion.36 = f32[2,512,2,128]{3,1,2,0:T(8,128)S(1)} fusion(f32[2,128,128,1]{2,1,0,3:T(8,128)S(1)} %bitcast.555, f32[1,512,128]{2,1,0:T(8,128)S(1)} %add.670, f32[1,512,128]{2,1,0:T(8,128)S(1)} %sub.388), kind=kOutput, calls=%fused_computation.52 | convolution fusion | flops 402784256 | bytes 1703936 | tf_op jit(solution)/shard_map/dot_general | solution.py:13
  67.3 1.0 %fusion.42 = f32[2,128,2,512]{3,1,2,0:T(8,128)S(1)} fusion(f32[2,128,128,1]{2,1,3,0:T(8,128)S(1)} %bitcast.561, f32[1,128,512]{2,1,0:T(8,128)S(1)} %stack.143, f32[1,128,512]{2,1,0:T(8,128)S(1)} %stack.142), kind=kOutput, calls=%fused_computation.60 | convolution fusion | flops 402784256 | bytes 1703936 | tf_op jit(solution)/shard_map/dot_general | solution.py:30
  68.4 1.9 %fusion.78 = (f32[1,4,128,128]{3,2,0,1:T(8,128)S(1)}, f32[1,4,128,128]{3,2,0,1:T(8,128)S(1)}) fusion(f32[1,4,128,128]{3,2,1,0:T(8,128)S(1)} %add.688, f32[1,4,128,128]{3,2,1,0:T(8,128)S(1)} %sub.394, f32[128,128]{1,0:T(8,128)S(1)} %bitcast.578, f32[4,128]{1,0:T(4,128)S(1)} %copy.41, f32[]{:T(128)} %bitcast.180), kind=kLoop, calls=%fused_computation.157 | loop fusion | flops 524288 | bytes 1116164 | tf_op jit(solution)/shard_map/sub | solution.py:44
  71.1 3.7 %all-to-all-start.2 = ((f32[2,4,128,128]{3,2,0,1:T(8,128)}), f32[2,4,128,128]{3,2,0,1:T(8,128)S(1)}, u32[]{:S(2)}, u32[]{:S(2)}) async-start(f32[2,4,128,128]{3,2,0,1:T(8,128)} %pad_maximum_fusion.2), calls=%async_computation.2 | async-start | bytes 1048576 | tf_op jit(solution)/shard_map/all_to_all | solution.py:59
  75.5 7.1 %all-to-all-done.2 = f32[2,4,128,128]{3,2,0,1:T(8,128)S(1)} async-done(((f32[2,4,128,128]{3,2,0,1:T(8,128)}), f32[2,4,128,128]{3,2,0,1:T(8,128)S(1)}, u32[]{:S(2)}, u32[]{:S(2)}) %all-to-all-start.2) | async-done | bytes 524320 | tf_op jit(solution)/shard_map/all_to_all | solution.py:59
  82.6 1.0 %fusion.120 = f32[2,512,2,128]{3,1,2,0:T(8,128)S(1)} fusion(f32[2,512,128,1]{2,1,3,0:T(8,128)S(1)} %bitcast.538, f32[2,128,128,1]{2,1,0,3:T(8,128)S(1)} %bitcast.558), kind=kOutput, calls=%fused_computation.287 | convolution fusion | flops 402653184 | bytes 1703936 | tf_op jit(solution)/shard_map/dot_general | solution.py:13
  88.2 1.0 %fusion.57 = f32[2,128,2,512]{3,1,2,0:T(8,128)S(1)} fusion(f32[2,128,128,1]{2,1,3,0:T(8,128)S(1)} %bitcast.564, f32[1,128,512]{2,1,0:T(8,128)S(1)} %stack.153, f32[1,128,512]{2,1,0:T(8,128)S(1)} %stack.152), kind=kOutput, calls=%fused_computation.81 | convolution fusion | flops 402784256 | bytes 1703936 | tf_op jit(solution)/shard_map/dot_general | solution.py:30
  90.4 1.3 %maximum_bitcast_fusion.40 = f32[2,65536]{1,0:T(2,128)} fusion(f32[1,1,65536]{2,0,1:T(1,128)S(1)} %get-tuple-element.57, f32[1,1,65536]{2,0,1:T(1,128)S(1)} %get-tuple-element.56), kind=kLoop, calls=%fused_computation.84 | loop fusion | flops 131072 | bytes 1048576 | tf_op jit(solution)/shard_map/reshape | solution.py:86
  (143 shorter events, 25.4 us)
Async XLA Ops:
  0.0 4.3 %copy-start = (f32[2,65536]{1,0:T(2,128)S(1)}, f32[2,65536]{1,0:T(2,128)}, u32[]{:S(2)}) copy-start(f32[2,65536]{1,0:T(2,128)} %param.5) | copy-start | bytes 1572868
  10.3 1.4 %copy-start.7 = (f32[128,128]{1,0:T(8,128)S(1)}, f32[128,128]{1,0:T(8,128)}, u32[]{:S(2)}) copy-start(f32[128,128]{1,0:T(8,128)} %get-tuple-element.14) | copy-start | bytes 196612
  10.3 1.4 %copy-start.8 = (f32[128,128]{1,0:T(8,128)S(1)}, f32[128,128]{1,0:T(8,128)}, u32[]{:S(2)}) copy-start(f32[128,128]{1,0:T(8,128)} %get-tuple-element.15) | copy-start | bytes 196612
  10.3 1.4 %copy-start.9 = (f32[128,128]{1,0:T(8,128)S(1)}, f32[128,128]{1,0:T(8,128)}, u32[]{:S(2)}) copy-start(f32[128,128]{1,0:T(8,128)} %get-tuple-element.18) | copy-start | bytes 196612
  10.4 1.4 %copy-start.10 = (f32[128,128]{1,0:T(8,128)S(1)}, f32[128,128]{1,0:T(8,128)}, u32[]{:S(2)}) copy-start(f32[128,128]{1,0:T(8,128)} %get-tuple-element.19) | copy-start | bytes 196612
  11.5 1.3 %copy-start.3 = (f32[128,128]{1,0:T(8,128)S(1)}, f32[128,128]{1,0:T(8,128)}, u32[]{:S(2)}) copy-start(f32[128,128]{1,0:T(8,128)} %get-tuple-element.26) | copy-start | bytes 196612
  11.5 1.3 %copy-start.4 = (f32[128,128]{1,0:T(8,128)S(1)}, f32[128,128]{1,0:T(8,128)}, u32[]{:S(2)}) copy-start(f32[128,128]{1,0:T(8,128)} %get-tuple-element.27) | copy-start | bytes 196612
  11.5 1.3 %copy-start.5 = (f32[128,128]{1,0:T(8,128)S(1)}, f32[128,128]{1,0:T(8,128)}, u32[]{:S(2)}) copy-start(f32[128,128]{1,0:T(8,128)} %get-tuple-element.28) | copy-start | bytes 196612
  11.6 1.3 %copy-start.6 = (f32[128,128]{1,0:T(8,128)S(1)}, f32[128,128]{1,0:T(8,128)}, u32[]{:S(2)}) copy-start(f32[128,128]{1,0:T(8,128)} %get-tuple-element.29) | copy-start | bytes 196612
  13.9 1.4 %copy-start.12 = (f32[4,256]{1,0:T(4,128)S(1)}, f32[4,256]{1,0:T(4,128)}, u32[]{:S(2)}) copy-start(f32[4,256]{1,0:T(4,128)} %param.8) | copy-start | bytes 12292
  14.0 1.6 %copy-start.13 = (f32[4,256]{1,0:T(4,128)S(1)}, f32[4,256]{1,0:T(4,128)}, u32[]{:S(2)}) copy-start(f32[4,256]{1,0:T(4,128)} %param.7) | copy-start | bytes 12292
  14.0 1.6 %copy-start.11 = (f32[4,1,1]{0,2,1:T(1,128)S(1)}, f32[4,1,1]{0,2,1:T(1,128)}, u32[]{:S(2)}) copy-start(f32[4,1,1]{0,2,1:T(1,128)} %param.9) | copy-start | bytes 52
  15.1 9.6 %copy-start.1 = (f32[128,128]{1,0:T(8,128)S(1)}, f32[128,128]{1,0:T(8,128)}, u32[]{:S(2)}) copy-start(f32[128,128]{1,0:T(8,128)} %get-tuple-element.32) | copy-start | bytes 196612
  15.1 9.6 %copy-start.2 = (f32[128,128]{1,0:T(8,128)S(1)}, f32[128,128]{1,0:T(8,128)}, u32[]{:S(2)}) copy-start(f32[128,128]{1,0:T(8,128)} %get-tuple-element.33) | copy-start | bytes 196612
  18.9 13.2 %all-to-all-start = ((f32[2,4,128,128]{3,2,0,1:T(8,128)}), f32[2,4,128,128]{3,2,0,1:T(8,128)S(1)}, u32[]{:S(2)}, u32[]{:S(2)}) async-start(f32[2,4,128,128]{3,2,0,1:T(8,128)} %pad_maximum_fusion), calls=%async_computation | async-start | bytes 1048576 | tf_op jit(solution)/shard_map/all_to_all | solution.py:59
  41.5 20.2 %all-to-all-start.1 = ((f32[2,8,64,128]{3,2,0,1:T(8,128)}), f32[2,8,64,128]{3,2,0,1:T(8,128)S(1)}, u32[]{:S(2)}, u32[]{:S(2)}) async-start(f32[2,8,64,128]{3,2,0,1:T(8,128)} %pad_maximum_fusion.1), calls=%async_computation.1 | async-start | bytes 1048576 | tf_op jit(solution)/shard_map/all_to_all | solution.py:63
  71.1 11.4 %all-to-all-start.2 = ((f32[2,4,128,128]{3,2,0,1:T(8,128)}), f32[2,4,128,128]{3,2,0,1:T(8,128)S(1)}, u32[]{:S(2)}, u32[]{:S(2)}) async-start(f32[2,4,128,128]{3,2,0,1:T(8,128)} %pad_maximum_fusion.2), calls=%async_computation.2 | async-start | bytes 1048576 | tf_op jit(solution)/shard_map/all_to_all | solution.py:59
where the time goes:
time: 92.3 us; the launch traced here: 91.7 us
  waiting for transfers between devices  26.9 us (29%)
  matrix products  24.5 us (27%)
  other arithmetic  14.6 us (16%)
  starting transfers between devices  13.8 us (15%)
  local copies, waits for them, and re-layouts  10.8 us (12%)
  between operations  1.1 us (1%)
    all_to_all x2, waiting for transfers between devices, regroup_with_gate(): lax.all_to_all(blocks, 'qa', split_axis=1, concat_axis=1, tiled=True)  14.5 us
    all_to_all x1, waiting for transfers between devices, regroup_with_gate(): lax.all_to_all(blocks, 'qb', split_axis=1, concat_axis=1, tiled=True)  12.4 us
    all_to_all x2, starting transfers between devices, regroup_with_gate(): lax.all_to_all(blocks, 'qa', split_axis=1, concat_axis=1, tiled=True)  8.92 us
    dot_general x8, matrix products, apply_gate(): lax.dot_general(values, stacked, (((1,), (1,)), ((), ())), precision=lax....  8.75 us
    dot_general x8, matrix products, apply_gate(): lax.dot_general(stacked, values, (((1,), (1,)), ((), ())), precision=lax....  7.86 us
    dot_general x8, matrix products, apply_gate(): lax.dot_general(stacked, values, (((1,), (2,)), ((), ())), precision=lax....  7.83 us
    sub x4, other arithmetic, apply_phase(): state[0] * cosine - state[1] * sine  5.94 us
    squeeze x3, local copies, waits for them, and re-layouts, apply_gate(): stacked = jnp.concatenate([matrix[0], matrix[1]], axis=0)  5.48 us
  transfers between devices with their start and end apart: 3, of which 3 were waited for; matrix products, arithmetic and copies ran while one was open for 4% of the time, Pallas kernels for 0%

commit v1 on v0

v1 whole, which is shorter than its diff:
```python
import functools

import jax
import jax.numpy as jnp
from jax import lax
from jax.experimental import pallas as pl
from jax.experimental.pallas import tpu as pltpu
from jax.sharding import PartitionSpec as P

F32 = jnp.float32
BF16 = jnp.bfloat16
SLAB = 16


def split(x):
    high = x.astype(BF16)
    return high, (x - high.astype(F32)).astype(BF16)


def dot(a, b):
    return jnp.dot(a, b, preferred_element_type=F32)


def dot3(ah, al, bh, bl):
    return dot(ah, bh) + (dot(al, bh) + dot(ah, bl))


def block_of(real, imag):
    top = jnp.concatenate([real, -imag], axis=1)
    low = jnp.concatenate([imag, real], axis=1)
    return jnp.concatenate([top, low], axis=0)


def inner_order(q, width, spect):
    group = SLAB * spect
    return (q // group) * group + (q % spect) * SLAB + (q % group) // spect


def one_hot(rows, cols, test):
    r = lax.broadcasted_iota(jnp.int32, (rows, cols), 0)
    c = lax.broadcasted_iota(jnp.int32, (rows, cols), 1)
    return jnp.where(test(r, c), 1.0, 0.0).astype(BF16)


def middle_weight(gate, spect, interleaved=False):
    width = gate.shape[-1]
    left = one_hot(width, width, lambda r, c: r == inner_order(c, width, spect))
    out = []
    for parts in zip(split(gate[0]), split(gate[1])):
        real = dot(left, parts[0]).astype(BF16)
        imag = dot(left, parts[1]).astype(BF16)
        if interleaved:
            right = one_hot(
                2 * width, 2 * width, lambda r, c: c == (r % width) * 2 + r // width
            )
            out.append(dot(block_of(real, imag), right).astype(BF16))
        else:
            right = one_hot(width, width, lambda r, c: c == inner_order(r, width, spect))
            real = dot(real, right).astype(BF16)
            imag = dot(imag, right).astype(BF16)
            out.append(block_of(real, imag))
    return out


def upper_weight(gate, cosine=None, sine=None):
    real, imag = gate[0], gate[1]
    if cosine is not None:
        real, imag = real * cosine - imag * sine, real * sine + imag * cosine
    return [block_of(r, i) for r, i in zip(split(real), split(imag))]


def lower_weight(first, second):
    width = first.shape[-1]
    lh, ll = split(jnp.concatenate([second[0], second[1]], axis=1))
    top = jnp.concatenate([first[0], first[1]], axis=1)
    low = jnp.concatenate([-first[1], first[0]], axis=1)
    rh, rl = split(jnp.concatenate([top, low], axis=0))
    joined = dot3(lh, ll, rh, rl)
    real, imag = joined[:, :width].T, joined[:, width:].T
    return [block_of(r, -i) for r, i in zip(split(real), split(imag))]


def weights(gates, spect, cosine, sine, first):
    return [
        lower_weight(gates[0], gates[3]),
        middle_weight(gates[1], spect, first),
        upper_weight(gates[2]),
        middle_weight(gates[4], spect),
        upper_weight(gates[5], cosine, sine),
    ]


def apply_lower(xh, xl, w):
    u, v, j, _, k, l = xh.shape
    rows = u * v * j * k

    def flat(x):
        return jnp.concatenate(
            [x[:, :, :, 0].reshape(rows, l), x[:, :, :, 1].reshape(rows, l)], axis=1
        )

    y = dot3(flat(xh), flat(xl), w[0], w[1])
    return y[:, :l].reshape(u, v, j, k, l), y[:, l:].reshape(u, v, j, k, l)


def columns(x, axis, at):
    u, v, j, _, k, l = x.shape
    out = []
    for one in at:
        part = x[one] if axis == 0 else x[:, :, one]
        a, b = part.shape[0], part.shape[1]
        real, imag = part[:, :, 0], part[:, :, 1]
        out.append(
            jnp.concatenate([real.reshape(a * b * k, l), imag.reshape(a * b * k, l)], axis=0)
        )
    return jnp.concatenate(out, axis=1)


def apply_rows(hi_ref, lo_ref, w, axis, done):
    u, v, j, _, k, l = hi_ref.shape
    count, inner = (u, (v, j)) if axis == 0 else (j, (u, v))
    half = inner[0] * inner[1] * k
    for at in range(0, count, 2):
        pair = (at, at + 1)

        def take(ref):
            out = []
            for one in pair:
                part = ref[one] if axis == 0 else ref[:, :, one]
                out.append(
                    jnp.concatenate(
                        [part[:, :, 0].reshape(half, l), part[:, :, 1].reshape(half, l)], axis=0
                    )
                )
            return jnp.concatenate(out, axis=1)

        y = dot3(w[0], w[1], take(hi_ref), take(lo_ref))
        for n, one in enumerate(pair):
            part = y[:, n * l : (n + 1) * l]
            done(one, part[:half].reshape(*inner, k, l), part[half:].reshape(*inner, k, l))


def keeper(hi_ref, lo_ref, axis):
    def keep(one, real, imag):
        for ri, value in ((0, real), (1, imag)):
            high, low = split(value)
            if axis == 0:
                hi_ref[one, :, :, ri] = high
                lo_ref[one, :, :, ri] = low
            else:
                hi_ref[:, :, one, ri] = high
                lo_ref[:, :, one, ri] = low

    return keep


def lower_in_place(hi_ref, lo_ref, w):
    real, imag = apply_lower(hi_ref[...], lo_ref[...], w)
    for ri, value in ((0, real), (1, imag)):
        high, low = split(value)
        hi_ref[:, :, :, ri] = high
        lo_ref[:, :, :, ri] = low


def first_kernel(spect, scalar_ref, x_ref, gate_ref, o_ref, hi_ref, lo_ref):
    u, v, j, _, k, l = hi_ref.shape
    w = weights(gate_ref[0], spect, scalar_ref[0, 0], scalar_ref[1, 0], True)
    block = 2 * v * j * k
    keep = keeper(hi_ref, lo_ref, 0)
    for at in range(0, u, 2):
        both = jnp.concatenate(
            [x_ref[at * block : (at + 1) * block], x_ref[(at + 1) * block : (at + 2) * block]],
            axis=1,
        )
        xh, xl = split(both)
        y = dot3(w[1][0], w[1][1], xh, xl)
        for n in range(2):
            part = y[:, n * l : (n + 1) * l]
            keep(
                at + n,
                part[: block // 2].reshape(v, j, k, l),
                part[block // 2 :].reshape(v, j, k, l),
            )
    apply_rows(hi_ref, lo_ref, w[2], 1, keeper(hi_ref, lo_ref, 1))
    apply_rows(hi_ref, lo_ref, w[3], 0, keeper(hi_ref, lo_ref, 0))
    lower_in_place(hi_ref, lo_ref, w[0])

    def put(one, real, imag):
        o_ref[:, :, one, 0] = real
        o_ref[:, :, one, 1] = imag

    apply_rows(hi_ref, lo_ref, w[4], 1, put)


def prepare_kernel(spect, scalar_ref, gate_ref, w_ref):
    at = pl.program_id(0) + 1
    made = weights(gate_ref[0], spect, scalar_ref[0, at], scalar_ref[1, at], False)
    for n, pair in enumerate(made):
        w_ref[0, n, 0] = pair[0]
        w_ref[0, n, 1] = pair[1]


def later_kernel(last, x_ref, e_ref, w_ref, *rest):
    if last:
        f_ref, o_ref, hi_ref, lo_ref = rest
    else:
        o_ref, hi_ref, lo_ref = rest
    u, v, j, _, k, l = hi_ref.shape
    eu, ev = e_ref.shape[0], e_ref.shape[1]
    for a in range(u):
        for b in range(v):
            c, s = e_ref[a % eu, b % ev, :, 0], e_ref[a % eu, b % ev, :, 1]
            real, imag = x_ref[a, b, :, 0], x_ref[a, b, :, 1]
            for ri, value in ((0, real * c - imag * s), (1, real * s + imag * c)):
                high, low = split(value)
                hi_ref[a, b, :, ri] = high
                lo_ref[a, b, :, ri] = low
    w = [(w_ref[0, n, 0], w_ref[0, n, 1]) for n in range(w_ref.shape[1])]
    lower_in_place(hi_ref, lo_ref, w[0])
    apply_rows(hi_ref, lo_ref, w[1], 0, keeper(hi_ref, lo_ref, 0))
    apply_rows(hi_ref, lo_ref, w[2], 1, keeper(hi_ref, lo_ref, 1))
    apply_rows(hi_ref, lo_ref, w[3], 0, keeper(hi_ref, lo_ref, 0))

    def put(one, real, imag):
        if not last:
            o_ref[:, :, one, 0] = real
            o_ref[:, :, one, 1] = imag
            return
        c, s = f_ref[:, :, one, 0], f_ref[:, :, one, 1]
        both = (real * c - imag * s, real * s + imag * c)
        stride = 2 * j
        for ri, value in enumerate(both):
            for a in range(u):
                for b in range(v):
                    start = (a * v + b) * k * stride + one * 2 + ri
                    o_ref[pl.ds(start, k, stride=stride), :] = value[a, b]

    apply_rows(hi_ref, lo_ref, w[4], 1, put)


def body(amplitudes, gate_blocks, phase_low, phase_high, phase_global):
    cells = amplitudes.shape[1]
    segments, per_segment, _, width, _ = gate_blocks.shape
    spect = cells // (width * width)
    k = SLAB
    v = width // spect // k
    dims = (spect, v, spect, 2, k, width)
    rows = 2 * cells // width
    highs = phase_high.shape[1]
    scalars = phase_global[:, 0, 0]
    scalars = jnp.stack([jnp.cos(scalars), jnp.sin(scalars)])
    smem = pl.BlockSpec(memory_space=pltpu.SMEM)
    vmem = pl.BlockSpec(memory_space=pltpu.VMEM)
    state_scratch = [pltpu.VMEM(dims, BF16), pltpu.VMEM(dims, BF16)]
    gate_shape = (1,) + gate_blocks.shape[1:]
    flops = 10 * 8 * cells * width

    x = amplitudes.reshape(2, cells // width, width).transpose(1, 0, 2).reshape(rows, width)
    state = pl.pallas_call(
        functools.partial(first_kernel, spect),
        out_shape=jax.ShapeDtypeStruct(dims, F32),
        grid=(1,),
        in_specs=[
            smem,
            pl.BlockSpec((rows, width), lambda i: (0, 0)),
            pl.BlockSpec(gate_shape, lambda i: (0, 0, 0, 0, 0)),
        ],
        out_specs=pl.BlockSpec(dims, lambda i: (0,) * 6),
        scratch_shapes=state_scratch,
        cost_estimate=pl.CostEstimate(flops=flops, bytes_accessed=16 * cells, transcendentals=0),
    )(scalars, x, gate_blocks)

    made = pl.pallas_call(
        functools.partial(prepare_kernel, spect),
        out_shape=jax.ShapeDtypeStruct((segments - 1, 5, 2, 2 * width, 2 * width), BF16),
        grid=(segments - 1,),
        in_specs=[smem, pl.BlockSpec(gate_shape, lambda i: (i + 1, 0, 0, 0, 0))],
        out_specs=pl.BlockSpec((1, 5, 2, 2 * width, 2 * width), lambda i: (i, 0, 0, 0, 0)),
        cost_estimate=pl.CostEstimate(
            flops=flops, bytes_accessed=16 * cells, transcendentals=0
        ),
    )(scalars, gate_blocks)

    def table(segment, count, index):
        high = phase_high[segment]
        if count > 1:
            high = lax.dynamic_slice_in_dim(high, index * (highs // count), highs // count)
            few = max(highs // count, k * (highs // (spect * v * k)))
            high = jnp.tile(high, few // (highs // count))
        upper = high.shape[0] // (k * 2)
        eu, ev = (upper // v, v) if upper >= v else (1, 1)
        low = phase_low[segment].reshape(2, width)
        high = high.reshape(eu, ev, k, spect // 2).transpose(0, 1, 3, 2)

        def grid(a, b):
            return a[:, :, :, None, :, None] * b[None, None, None, :, None, :]

        ch, sh, cl, sl = jnp.cos(high), jnp.sin(high), jnp.cos(low), jnp.sin(low)
        cosine = grid(ch, cl) - grid(sh, sl)
        sine = grid(sh, cl) + grid(ch, sl)
        both = jnp.stack([cosine, sine], axis=4)
        return both.reshape(eu, ev, spect, 2, k, width)

    def exchange(value, name):
        count = lax.axis_size(name)
        tops = spect * v
        if count <= tops:
            blocks = value.reshape(count, rows // count, width)
            moved = lax.all_to_all(blocks, name, split_axis=0, concat_axis=0, tiled=True)
            return moved.reshape(dims)
        more = count // tops
        blocks = value.reshape(tops, spect * 2, more, k // more, width)
        blocks = blocks.transpose(0, 2, 1, 3, 4).reshape(count, rows // count, width)
        moved = lax.all_to_all(blocks, name, split_axis=0, concat_axis=0, tiled=True)
        moved = moved.reshape(tops, more, spect * 2, k // more, width)
        return moved.transpose(0, 2, 1, 3, 4).reshape(dims)

    final = table(segments - 1, 1, 0)
    for segment in range(1, segments):
        name = "qb" if segment == 2 else "qa"
        state = exchange(state, name)
        entry = table(segment - 1, lax.axis_size(name), lax.axis_index(name))
        last = segment == segments - 1
        extra = [final] if last else []
        out = (rows, width) if last else dims
        state = pl.pallas_call(
            functools.partial(later_kernel, last),
            out_shape=jax.ShapeDtypeStruct(out, F32),
            grid=(1,),
            in_specs=[
                pl.BlockSpec(dims, lambda i: (0,) * 6),
                pl.BlockSpec(entry.shape, lambda i: (0,) * 6),
                pl.BlockSpec(
                    (1, 5, 2, 2 * width, 2 * width), lambda i, s=segment: (s - 1, 0, 0, 0, 0)
                ),
            ]
            + [pl.BlockSpec(f.shape, lambda i: (0,) * 6) for f in extra],
            out_specs=pl.BlockSpec(out, lambda i, n=len(out): (0,) * n),
            scratch_shapes=state_scratch,
            cost_estimate=pl.CostEstimate(
                flops=flops, bytes_accessed=24 * cells, transcendentals=0
            ),
        )(state, entry, made, *extra)
    return state.reshape(cells // width, 2, width).transpose(1, 0, 2).reshape(2, cells)


def solution(mesh):
    return jax.shard_map(
        body,
        mesh=mesh,
        in_specs=(P(None, ("qa", "qb")), P(), P(), P(), P(None, "qa", "qb")),
        out_specs=P(None, ("qa", "qb")),
        check_vma=False,
    )
```

time: 92.3 us -> 67.6 us (0.73)
  matrix products: 24.5 us -> 0 us
  Pallas kernels: 0 us -> 23.9 us
  other arithmetic: 14.6 us -> 3.84 us
  waiting for transfers between devices: 26.9 us -> 20.4 us
  local copies, waits for them, and re-layouts: 10.8 us -> 5.21 us
  between operations: 1.1 us -> 0.16 us
    dot_general x24 -> x0, matrix products: 24.5 us -> none  [the longest x8 8.75 us: apply_gate(): lax.dot_general(values, stacked, (((1,), (1,)), ((), ())), precision=lax....]
    pallas_call x0 -> x5, Pallas kernels: none -> 23.9 us  [the longest x3 13.7 us: body(): pl.pallas_call(functools.partial(later_kernel, last), out_shape=jax.Shape...]
    sub x20 -> x4, other arithmetic: 7.52 us -> 0.49 us  [table(): cosine = grid(ch, cl) - grid(sh, sl)]
    all_to_all x3, waiting for transfers between devices: 26.9 us -> 20.4 us  [exchange(): lax.all_to_all(blocks, name, split_axis=0, concat_axis=0, tiled=True)]
    squeeze x3 -> x0, local copies, waits for them, and re-layouts: 5.48 us -> none  [apply_gate(): stacked = jnp.concatenate([matrix[0], matrix[1]], axis=0)]
    unnamed x28 -> x10, local copies, waits for them, and re-layouts: 0.07 us -> 2.39 us
    cos x1 -> x13, local copies, waits for them, and re-layouts: 0.26 us -> 1.98 us  [the longest x12 1.26 us: table(): ch, sh, cl, sl = (jnp.cos(high), jnp.sin(high), jnp.cos(low), jnp.sin(low))]
    sin x1 -> x0, other arithmetic: 1.63 us -> none  [apply_phase(): sine = jnp.sin(theta)]
  transfers between devices with their start and end apart: 3 -> 3, of which waited for: 3 -> 3; matrix products, arithmetic and copies ran while one was open for 4% -> 8% of each run, Pallas kernels for 0% -> 8%
where the time goes in v1:
time: 67.6 us; the launch traced here: 67 us
  Pallas kernels  23.9 us (35%)
  waiting for transfers between devices  20.4 us (30%)
  starting transfers between devices  13.5 us (20%)
  local copies, waits for them, and re-layouts  5.21 us (8%)
  other arithmetic  3.84 us (6%)
    all_to_all x3, waiting for transfers between devices, exchange(): lax.all_to_all(blocks, name, split_axis=0, concat_axis=0, tiled=True)  20.4 us
    pallas_call x3, Pallas kernels, body(): pl.pallas_call(functools.partial(later_kernel, last), out_shape=jax.Shape...  13.7 us
    all_to_all x3, starting transfers between devices, exchange(): lax.all_to_all(blocks, name, split_axis=0, concat_axis=0, tiled=True)  13.5 us
    pallas_call x1, Pallas kernels, body(): pl.pallas_call(functools.partial(prepare_kernel, spect), out_shape=jax.Sh...  5.35 us
    pallas_call x1, Pallas kernels, body(): pl.pallas_call(functools.partial(first_kernel, spect), out_shape=jax.Shap...  4.78 us
    another operation x4, other arithmetic, table(): both = jnp.stack([cosine, sine], axis=4)  2.78 us
    unnamed x10, local copies, waits for them, and re-layouts  2.39 us
  transfers between devices with their start and end apart: 3, of which 3 were waited for; matrix products, arithmetic and copies ran while one was open for 8% of the time, Pallas kernels for 8%

profile of v1, /device:TPU:0, one launch (start us, length us, event | category | flops | bytes accessed | tf_op | source)
XLA Modules:
  0.0 67.0 jit_solution(3956560253674208377)
XLA Ops:
  0.0 0.7 %cosine_bitcast_fusion = (f32[1,4]{1,0:T(1,128)S(1)}, f32[1,4]{1,0:T(1,128)S(1)}) fusion(f32[4,1,1]{0,2,1:T(1,128)} %param.9), kind=kLoop, calls=%fused_computation.33 | loop fusion | bytes 48 | tf_op jit(solution)/shard_map/cos | solution.py:251
  0.7 0.6 pad_maximum_fusion.4.scalar_ref
  1.3 4.8 %shard_map.55 = f32[4,2,4,2,16,128]{5,4,3,2,1,0:T(8,128)} custom-call(f32[2,4]{1,0:T(2,128)} %pad_maximum_fusion.4.scalar_ref, f32[1024,128]{1,0:T(8,128)} %bitcast.64, f32[4,6,2,128,128]{4,3,2,1,0:T(8,128)} %gate_ref.3), custom_call_target="tpu_custom_call" | custom-call | flops 671088640 | bytes 1048576 | tf_op jit(solution)/shard_map/pallas_call | solution.py:259
  6.1 5.2 %all-to-all-start = ((f32[4,256,128]{2,1,0:T(8,128)}), f32[4,256,128]{2,1,0:T(8,128)S(1)}, u32[]{:S(2)}, u32[]{:S(2)}) async-start(f32[4,256,128]{2,1,0:T(8,128)} %bitcast.61), calls=%async_computation | async-start | bytes 1048576 | tf_op jit(solution)/shard_map/all_to_all | solution.py:309
  11.3 0.1 cosine_reduce_fusion.1
  11.9 0.1 slice_cosine_fusion
  12.0 5.3 %shard_map.56.w_ref = bf16[3,5,2,256,256]{4,3,2,1,0:T(8,128)(2,1)} custom-call(f32[2,4]{1,0:T(2,128)} %pad_maximum_fusion.4.scalar_ref, f32[4,6,2,128,128]{4,3,2,1,0:T(8,128)} %gate_ref.3), custom_call_target="tpu_custom_call" | custom-call | flops 671088640 | bytes 1048576 | tf_op jit(solution)/shard_map/pallas_call | solution.py:273
  17.5 0.7 pad_maximum_fusion.1.e_ref
  18.1 1.1 %all-to-all-done = f32[4,256,128]{2,1,0:T(8,128)S(1)} async-done(((f32[4,256,128]{2,1,0:T(8,128)}), f32[4,256,128]{2,1,0:T(8,128)S(1)}, u32[]{:S(2)}, u32[]{:S(2)}) %all-to-all-start) | async-done | bytes 524320 | tf_op jit(solution)/shard_map/all_to_all | solution.py:309
  19.3 0.8 %copy-done.1 = f32[4,256,128]{2,1,0:T(8,128)} copy-done((f32[4,256,128]{2,1,0:T(8,128)}, f32[4,256,128]{2,1,0:T(8,128)S(1)}, u32[]{:S(2)}) %copy-start.1) | copy-done | bytes 524312
  20.1 4.5 %shard_map.57 = f32[4,2,4,2,16,128]{5,4,3,2,1,0:T(8,128)} custom-call(f32[4,2,4,2,16,128]{5,4,3,2,1,0:T(8,128)} %bitcast.60, f32[1,2,4,2,16,128]{5,4,3,2,1,0:T(8,128)} %pad_maximum_fusion.1.e_ref, bf16[3,5,2,256,256]{4,3,2,1,0:T(8,128)(2,1)} %shard_map.56.w_ref), custom_call_target="tpu_custom_call" | custom-call | flops 671088640 | bytes 1572864 | tf_op jit(solution)/shard_map/pallas_call | solution.py:326
  24.6 4.9 %all-to-all-start.1 = ((f32[8,128,128]{2,1,0:T(8,128)}), f32[8,128,128]{2,1,0:T(8,128)S(1)}, u32[]{:S(2)}, u32[]{:S(2)}) async-start(f32[8,128,128]{2,1,0:T(8,128)} %bitcast.59), calls=%async_computation.1 | async-start | bytes 1048576 | tf_op jit(solution)/shard_map/all_to_all | solution.py:309
  30.5 0.6 pad_maximum_fusion.3.e_ref
  31.2 13.6 %all-to-all-done.1 = f32[8,128,128]{2,1,0:T(8,128)S(1)} async-done(((f32[8,128,128]{2,1,0:T(8,128)}), f32[8,128,128]{2,1,0:T(8,128)S(1)}, u32[]{:S(2)}, u32[]{:S(2)}) %all-to-all-start.1) | async-done | bytes 524320 | tf_op jit(solution)/shard_map/all_to_all | solution.py:309
  44.8 0.8 %copy-done = f32[8,128,128]{2,1,0:T(8,128)} copy-done((f32[8,128,128]{2,1,0:T(8,128)}, f32[8,128,128]{2,1,0:T(8,128)S(1)}, u32[]{:S(2)}) %copy-start) | copy-done | bytes 524312
  45.6 4.5 %shard_map.58 = f32[4,2,4,2,16,128]{5,4,3,2,1,0:T(8,128)} custom-call(f32[4,2,4,2,16,128]{5,4,3,2,1,0:T(8,128)} %bitcast.58, f32[1,1,4,2,16,128]{5,4,3,2,1,0:T(8,128)} %pad_maximum_fusion.3.e_ref, bf16[3,5,2,256,256]{4,3,2,1,0:T(8,128)(2,1)} %shard_map.56.w_ref), custom_call_target="tpu_custom_call" | custom-call | flops 671088640 | bytes 1572864 | tf_op jit(solution)/shard_map/pallas_call | solution.py:326
  50.1 3.5 %all-to-all-start.2 = ((f32[4,256,128]{2,1,0:T(8,128)}), f32[4,256,128]{2,1,0:T(8,128)S(1)}, u32[]{:S(2)}, u32[]{:S(2)}) async-start(f32[4,256,128]{2,1,0:T(8,128)} %bitcast.62), calls=%async_computation.2 | async-start | bytes 1048576 | tf_op jit(solution)/shard_map/all_to_all | solution.py:309
  53.6 0.7 pad_maximum_fusion.2.e_ref
  54.5 0.1 sin.107
  54.8 0.2 multiply_subtract_fusion
  55.0 0.8 %pad_maximum_fusion.rest_0_ = f32[4,2,4,2,16,128]{5,4,3,2,1,0:T(8,128)} fusion(f32[4,2,4,1,16,128]{5,4,3,2,1,0:T(8,128)S(1)} %get-tuple-element.14, f32[4,2,4,1,16,128]{5,4,3,2,1,0:T(8,128)S(1)} %get-tuple-element.13), kind=kLoop, calls=%fused_computation | loop fusion | flops 131072 | bytes 1048576 | tf_op jit(solution)/shard_map/stack | solution.py:301
  55.8 5.7 %all-to-all-done.2 = f32[4,256,128]{2,1,0:T(8,128)S(1)} async-done(((f32[4,256,128]{2,1,0:T(8,128)}), f32[4,256,128]{2,1,0:T(8,128)S(1)}, u32[]{:S(2)}, u32[]{:S(2)}) %all-to-all-start.2) | async-done | bytes 524320 | tf_op jit(solution)/shard_map/all_to_all | solution.py:309
  61.5 0.8 %copy-done.2 = f32[4,256,128]{2,1,0:T(8,128)} copy-done((f32[4,256,128]{2,1,0:T(8,128)}, f32[4,256,128]{2,1,0:T(8,128)S(1)}, u32[]{:S(2)}) %copy-start.2) | copy-done | bytes 524312
  62.3 4.7 %shard_map.59 = f32[1024,128]{1,0:T(8,128)} custom-call(f32[4,2,4,2,16,128]{5,4,3,2,1,0:T(8,128)} %bitcast.63, f32[1,2,4,2,16,128]{5,4,3,2,1,0:T(8,128)} %pad_maximum_fusion.2.e_ref, bf16[3,5,2,256,256]{4,3,2,1,0:T(8,128)(2,1)} %shard_map.56.w_ref, f32[4,2,4,2,16,128]{5,4,3,2,1,0:T(8,128)} %pad_maximum_fusion.rest_0_), custom_call_target="tpu_custom_call" | custom-call | flops 671088640 | bytes 1572864 | tf_op jit(solution)/shard_map/pallas_call | solution.py:326
  (43 shorter events, 2.0 us)
Async XLA Ops:
  0.0 11.3 %copy-start.4 = (f32[4,256]{1,0:T(4,128)S(1)}, f32[4,256]{1,0:T(4,128)}, u32[]{:S(2)}) copy-start(f32[4,256]{1,0:T(4,128)} %param.8) | copy-start | bytes 12292
  0.0 11.9 %copy-start.3 = (f32[4,256]{1,0:T(4,128)S(1)}, f32[4,256]{1,0:T(4,128)}, u32[]{:S(2)}) copy-start(f32[4,256]{1,0:T(4,128)} %param.7) | copy-start | bytes 12292
  6.1 13.2 %all-to-all-start = ((f32[4,256,128]{2,1,0:T(8,128)}), f32[4,256,128]{2,1,0:T(8,128)S(1)}, u32[]{:S(2)}, u32[]{:S(2)}) async-start(f32[4,256,128]{2,1,0:T(8,128)} %bitcast.61), calls=%async_computation | async-start | bytes 1048576 | tf_op jit(solution)/shard_map/all_to_all | solution.py:309
  19.3 0.8 %copy-start.1 = (f32[4,256,128]{2,1,0:T(8,128)}, f32[4,256,128]{2,1,0:T(8,128)S(1)}, u32[]{:S(2)}) copy-start(f32[4,256,128]{2,1,0:T(8,128)S(1)} %all-to-all-done) | copy-start | bytes 1572868
  24.6 20.2 %all-to-all-start.1 = ((f32[8,128,128]{2,1,0:T(8,128)}), f32[8,128,128]{2,1,0:T(8,128)S(1)}, u32[]{:S(2)}, u32[]{:S(2)}) async-start(f32[8,128,128]{2,1,0:T(8,128)} %bitcast.59), calls=%async_computation.1 | async-start | bytes 1048576 | tf_op jit(solution)/shard_map/all_to_all | solution.py:309
  44.8 0.8 %copy-start = (f32[8,128,128]{2,1,0:T(8,128)}, f32[8,128,128]{2,1,0:T(8,128)S(1)}, u32[]{:S(2)}) copy-start(f32[8,128,128]{2,1,0:T(8,128)S(1)} %all-to-all-done.1) | copy-start | bytes 1572868
  50.1 11.4 %all-to-all-start.2 = ((f32[4,256,128]{2,1,0:T(8,128)}), f32[4,256,128]{2,1,0:T(8,128)S(1)}, u32[]{:S(2)}, u32[]{:S(2)}) async-start(f32[4,256,128]{2,1,0:T(8,128)} %bitcast.62), calls=%async_computation.2 | async-start | bytes 1048576 | tf_op jit(solution)/shard_map/all_to_all | solution.py:309
  61.5 0.8 %copy-start.2 = (f32[4,256,128]{2,1,0:T(8,128)}, f32[4,256,128]{2,1,0:T(8,128)S(1)}, u32[]{:S(2)}) copy-start(f32[4,256,128]{2,1,0:T(8,128)S(1)} %all-to-all-done.2) | copy-start | bytes 1572868
